TPU v7x, 32 devices: a whole 2x2x4 slice. The times are simulated.
32 devices in a mesh: group: 4 (over z), replica: 8 (over y, x, core).
Axes of the slice: x: 2, y: 2, z: 4, core: 2. Of those that a mesh axis runs over, the one named last changes fastest.
Arguments:
- layer_input: bfloat16 [8, 1024, 2560], P('replica', 'group')
- positions: int32 [8, 1024], P('replica', 'group'), may hold values from 0 to 543, as said below
- piece_starts: int32 [8, 2], P('replica'), may hold values from 0 to 768, as said below
- gain_attn: bfloat16 [2560], P('group'), may hold values from 0.5 to 1.5
- w_query: bfloat16 [2560, 2560], P('group'), may hold values from -0.125 to 0.125
- w_key: bfloat16 [2560, 640], P('group'), may hold values from -0.125 to 0.125
- w_value: bfloat16 [2560, 640], P('group'), may hold values from -0.125 to 0.125
- w_out: bfloat16 [2560, 2560], P('group'), may hold values from -2 to 2
- gain_mlp: bfloat16 [2560], P('group'), may hold values from 0.5 to 1.5
- w_gate: bfloat16 [2560, 7168], P('group'), may hold values from -0.125 to 0.125
- w_up: bfloat16 [2560, 7168], P('group'), may hold values from -0.125 to 0.125
- w_down: bfloat16 [2560, 7168], P('group'), may hold values from -0.0625 to 0.0625
- out_grad: bfloat16 [8, 1024, 2560], P('replica', 'group'), may hold values from -6 to 6
Outputs:
- layer_out: bfloat16 [8, 1024, 2560], P('replica', 'group')
- input_grad: float32 [8, 1024, 2560], P('replica', 'group')
- grad_norm_attn: float32 [2560], P(('group', 'replica'))
- grad_query: float32 [2560, 2560], P(('group', 'replica'))
- grad_key: float32 [2560, 640], P(('group', 'replica'))
- grad_value: float32 [2560, 640], P(('group', 'replica'))
- grad_out: float32 [2560, 2560], P(('group', 'replica'))
- grad_norm_mlp: float32 [2560], P(('group', 'replica'))
- grad_gate: float32 [2560, 7168], P(('group', 'replica'))
- grad_up: float32 [2560, 7168], P(('group', 'replica'))
- grad_down: float32 [2560, 7168], P(('group', 'replica'))
- stream_rms: float32 [8, 3], P('replica')
Inputs may be any that keep to these rules, and one draw needn't show every extreme that they name: `piece_starts`: each sequence holds two picture pieces of 256 tokens that start at multiples of 128, the second starting 256 or more tokens after the first, both ending inside the sequence. `positions`: outside picture pieces a token's position is one more than the previous token's; the j-th token of a piece whose first token has position p gets p + j // 16, and the token after the piece gets p + 16; a sequence's first token has position 0.
All inputs are finite; a program needn't handle non-finite values.
Results may differ from a plain program's by a relative error of at most 0.018.
Values may be sent and summed in bfloat16 or wider, within the bound.
No kernel may reach another device: no remote copies, remote signals or barrier semaphores. Data moves between devices by JAX's collectives and lax.ppermute only.
A program may use at most 384 MiB of HBM per device.

v0:
```python
import jax
import jax.numpy as jnp
from jax import lax
from jax.sharding import PartitionSpec as P

HEADS = 32
KV_HEADS = 8
HEAD_DIM = 80
PIECE = 256
epsilon = 1e-05
rope_base = 1000000.0


def rope_tables(places):
    halves = HEAD_DIM // 2
    frequency = rope_base ** (-(jnp.arange(halves, dtype=jnp.float32) * 2.0 / HEAD_DIM))
    angles = places.astype(jnp.float32)[..., None] * frequency
    angles = jnp.concatenate([angles, angles], axis=-1)
    return (jnp.cos(angles), jnp.sin(angles))


def rotate(values, cosine, sine):
    halves = HEAD_DIM // 2
    turned = jnp.concatenate([-values[..., halves:], values[..., :halves]], axis=-1)
    return values * cosine[:, :, None, :] + turned * sine[:, :, None, :]


def unrotate(grads, cosine, sine):
    halves = HEAD_DIM // 2
    shifted = grads * sine[:, :, None, :]
    turned = jnp.concatenate([shifted[..., halves:], -shifted[..., :halves]], axis=-1)
    return grads * cosine[:, :, None, :] + turned


def times_t(left, right):
    return lax.dot_general(
        left, right, (((1,), (1,)), ((), ())), preferred_element_type=jnp.float32
    )


def inner_t(left, right):
    return lax.dot_general(
        left, right, (((0,), (0,)), ((), ())), preferred_element_type=jnp.float32
    )


def inverse_rms(values):
    return lax.rsqrt(jnp.mean(values * values, axis=-1, keepdims=True) + epsilon)


def norm_back(grad_normed, source, inverse, gain_full):
    weighted = grad_normed * gain_full
    average = jnp.mean(weighted * source, axis=-1, keepdims=True)
    return inverse * weighted - source * (inverse * inverse * inverse) * average


def piece_index(starts, places):
    labels = jnp.zeros(places.shape, jnp.int32)
    for which in range(2):
        inside = (places >= starts[which]) & (places < starts[which] + PIECE)
        labels = jnp.where(inside, which + 1, labels)
    return labels


def shards(
    layer_input,
    positions,
    piece_starts,
    gain_attn,
    w_query,
    w_key,
    w_value,
    w_out,
    gain_mlp,
    w_gate,
    w_up,
    w_down,
    out_grad,
):
    sequences, block_size, model_width = layer_input.shape
    token_rows = sequences * block_size
    kv_width = KV_HEADS * HEAD_DIM
    repeats = HEADS // KV_HEADS
    scaling = HEAD_DIM ** (-0.5)
    full_len = block_size * lax.axis_size("group")
    source = layer_input.astype(jnp.float32).reshape(token_rows, model_width)
    inverse_one = inverse_rms(source)
    unit_one = source * inverse_one
    gain_piece = lax.all_gather(gain_attn, "group", axis=0, tiled=True)
    query_piece = lax.all_gather(w_query, "group", axis=0, tiled=True)
    key_piece = lax.all_gather(w_key, "group", axis=0, tiled=True)
    value_piece = lax.all_gather(w_value, "group", axis=0, tiled=True)
    out_piece = lax.all_gather(w_out, "group", axis=0, tiled=True)
    scaled = unit_one * gain_piece.astype(jnp.float32)
    scaled = scaled.astype(jnp.bfloat16)
    query = jnp.dot(scaled, query_piece, preferred_element_type=jnp.float32)
    keyed = jnp.dot(scaled, key_piece, preferred_element_type=jnp.float32)
    valued = jnp.dot(scaled, value_piece, preferred_element_type=jnp.float32)
    normed = scaled
    gains = gain_piece
    out_full = out_piece
    query_lin, key_lin, value_lin, normed_one, gain_one_low, out_full = (
        query,
        keyed,
        valued,
        normed,
        gains,
        out_full,
    )
    gain_one = gain_one_low.astype(jnp.float32)
    cosine, sine = rope_tables(positions)
    query_rot = rotate(
        query_lin.reshape(sequences, block_size, HEADS, HEAD_DIM), cosine, sine
    ).astype(jnp.bfloat16)
    key_rot = rotate(
        key_lin.reshape(sequences, block_size, KV_HEADS, HEAD_DIM), cosine, sine
    ).astype(jnp.bfloat16)
    key_rot = key_rot.reshape(sequences, block_size, kv_width)
    value_low = value_lin.astype(jnp.bfloat16).reshape(sequences, block_size, kv_width)
    key_all, value_all = (
        lax.all_gather(key_rot, "group", axis=1, tiled=True),
        lax.all_gather(value_low, "group", axis=1, tiled=True),
    )
    query_places = lax.axis_index("group") * block_size + jnp.arange(block_size, dtype=jnp.int32)
    key_places = jnp.arange(full_len, dtype=jnp.int32)

    def allowed_for(starts):
        query_labels = piece_index(starts, query_places)
        key_labels = piece_index(starts, key_places)
        causal = key_places[None, :] <= query_places[:, None]
        same_piece = (query_labels[:, None] == key_labels[None, :]) & (query_labels[:, None] > 0)
        return causal | same_piece

    def scores_of(query_seq, key_seq, starts):
        grouped = query_seq.reshape(block_size, KV_HEADS, repeats, HEAD_DIM)
        keys_grouped = key_seq.reshape(full_len, KV_HEADS, HEAD_DIM)
        raw = (
            jnp.einsum("qkrd,skd->krqs", grouped, keys_grouped, preferred_element_type=jnp.float32)
            * scaling
        )
        return jnp.where(allowed_for(starts)[None, None], raw, -1e30)

    def attend_one(packed):
        query_seq, key_seq, value_seq, starts = packed
        masked = scores_of(query_seq, key_seq, starts)
        highest_score = jnp.max(masked, axis=-1, keepdims=True)
        raised = jnp.exp(masked - highest_score)
        summed = jnp.sum(raised, axis=-1, keepdims=True)
        chances_low = (raised / summed).astype(jnp.bfloat16)
        values_grouped = value_seq.reshape(full_len, KV_HEADS, HEAD_DIM)
        mixed = jnp.einsum(
            "krqs,skd->qkrd", chances_low, values_grouped, preferred_element_type=jnp.float32
        )
        return (mixed.reshape(block_size, model_width), highest_score + jnp.log(summed))

    mixed_all, log_totals = lax.map(attend_one, (query_rot, key_all, value_all, piece_starts))
    mixed_low = mixed_all.reshape(token_rows, model_width).astype(jnp.bfloat16)
    middle = source + times_t(mixed_low, out_full)
    inverse_two = inverse_rms(middle)
    unit_two = middle * inverse_two
    gain_piece = lax.all_gather(gain_mlp, "group", axis=0, tiled=True)
    gate_piece = lax.all_gather(w_gate, "group", axis=0, tiled=True)
    up_piece = lax.all_gather(w_up, "group", axis=0, tiled=True)
    down_piece = lax.all_gather(w_down, "group", axis=0, tiled=True)
    scaled = unit_two * gain_piece.astype(jnp.float32)
    scaled = scaled.astype(jnp.bfloat16)
    gated = jnp.dot(scaled, gate_piece, preferred_element_type=jnp.float32)
    lifted = jnp.dot(scaled, up_piece, preferred_element_type=jnp.float32)
    normed = scaled
    gains = gain_piece
    down_full = down_piece
    gated, lifted, normed_two, gain_two_low, down_full = (gated, lifted, normed, gains, down_full)
    gain_two = gain_two_low.astype(jnp.float32)
    activated = jax.nn.silu(gated)
    hidden = (activated * lifted).astype(jnp.bfloat16)
    output_full = middle + times_t(hidden, down_full)
    grad_low = out_grad.reshape(token_rows, model_width)
    grad_top = grad_low.astype(jnp.float32)
    grad_hidden = jnp.dot(grad_low, down_full, preferred_element_type=jnp.float32)
    sigmoid_gate = jax.nn.sigmoid(gated)
    grad_gate_low = (
        grad_hidden * lifted * (sigmoid_gate + gated * sigmoid_gate * (1.0 - sigmoid_gate))
    ).astype(jnp.bfloat16)
    grad_lift_low = (grad_hidden * activated).astype(jnp.bfloat16)
    gate_piece = lax.all_gather(w_gate, "group", axis=0, tiled=True)
    up_piece = lax.all_gather(w_up, "group", axis=0, tiled=True)
    added = times_t(grad_gate_low, gate_piece) + times_t(grad_lift_low, up_piece)
    grad_normed_two = added
    grad_gain_two = jnp.sum(grad_normed_two * unit_two, axis=0)
    grad_middle = grad_top + norm_back(grad_normed_two, middle, inverse_two, gain_two)
    grad_middle_low = grad_middle.astype(jnp.bfloat16)
    grad_mixed_low = jnp.dot(grad_middle_low, out_full, preferred_element_type=jnp.float32).astype(
        jnp.bfloat16
    )

    def attend_back(packed):
        query_seq, key_seq, value_seq, starts, log_total, grad_seq = packed
        masked = scores_of(query_seq, key_seq, starts)
        chances = jnp.exp(masked - log_total)
        grad_grouped = grad_seq.reshape(block_size, KV_HEADS, repeats, HEAD_DIM)
        values_grouped = value_seq.reshape(full_len, KV_HEADS, HEAD_DIM)
        keys_grouped = key_seq.reshape(full_len, KV_HEADS, HEAD_DIM)
        query_grouped = query_seq.reshape(block_size, KV_HEADS, repeats, HEAD_DIM)
        grad_value_seq = jnp.einsum(
            "krqs,qkrd->skd",
            chances.astype(jnp.bfloat16),
            grad_grouped,
            preferred_element_type=jnp.float32,
        )
        grad_chance = jnp.einsum(
            "qkrd,skd->krqs", grad_grouped, values_grouped, preferred_element_type=jnp.float32
        )
        grad_score = chances * (
            grad_chance - jnp.sum(chances * grad_chance, axis=-1, keepdims=True)
        )
        grad_score = grad_score.astype(jnp.bfloat16)
        grad_query_seq = (
            jnp.einsum(
                "krqs,skd->qkrd", grad_score, keys_grouped, preferred_element_type=jnp.float32
            )
            * scaling
        )
        grad_key_seq = (
            jnp.einsum(
                "krqs,qkrd->skd", grad_score, query_grouped, preferred_element_type=jnp.float32
            )
            * scaling
        )
        return (
            grad_query_seq.reshape(block_size, HEADS, HEAD_DIM),
            grad_key_seq.reshape(full_len, kv_width),
            grad_value_seq.reshape(full_len, kv_width),
        )

    grad_query_rot, grad_key_full, grad_value_full = lax.map(
        attend_back,
        (
            query_rot,
            key_all,
            value_all,
            piece_starts,
            log_totals,
            grad_mixed_low.reshape(sequences, block_size, model_width),
        ),
    )
    grad_key_rot, grad_value_sum = (
        lax.psum_scatter(grad_key_full, "group", scatter_dimension=1, tiled=True),
        lax.psum_scatter(grad_value_full, "group", scatter_dimension=1, tiled=True),
    )
    grad_query_low = (
        unrotate(grad_query_rot, cosine, sine).astype(jnp.bfloat16).reshape(token_rows, model_width)
    )
    grad_key_low = (
        unrotate(grad_key_rot.reshape(sequences, block_size, KV_HEADS, HEAD_DIM), cosine, sine)
        .astype(jnp.bfloat16)
        .reshape(token_rows, kv_width)
    )
    grad_value_low = grad_value_sum.astype(jnp.bfloat16).reshape(token_rows, kv_width)
    query_piece = lax.all_gather(w_query, "group", axis=0, tiled=True)
    key_piece = lax.all_gather(w_key, "group", axis=0, tiled=True)
    value_piece = lax.all_gather(w_value, "group", axis=0, tiled=True)
    added = (
        times_t(grad_query_low, query_piece)
        + times_t(grad_key_low, key_piece)
        + times_t(grad_value_low, value_piece)
    )
    grad_gain_one = jnp.sum(added * unit_one, axis=0)
    input_grad = grad_middle + norm_back(added, source, inverse_one, gain_one)
    normed_own, middle_own, normed_mlp_own, top_own = (
        lax.all_to_all(normed_one, "group", split_axis=1, concat_axis=0, tiled=True),
        lax.all_to_all(grad_middle_low, "group", split_axis=1, concat_axis=0, tiled=True),
        lax.all_to_all(normed_two, "group", split_axis=1, concat_axis=0, tiled=True),
        lax.all_to_all(grad_low, "group", split_axis=1, concat_axis=0, tiled=True),
    )
    query_rows, key_rows, value_rows, mixed_rows = (
        lax.all_gather(grad_query_low, "group", axis=0, tiled=True),
        lax.all_gather(grad_key_low, "group", axis=0, tiled=True),
        lax.all_gather(grad_value_low, "group", axis=0, tiled=True),
        lax.all_gather(mixed_low, "group", axis=0, tiled=True),
    )
    gate_rows, lift_rows, hidden_rows = (
        lax.all_gather(grad_gate_low, "group", axis=0, tiled=True),
        lax.all_gather(grad_lift_low, "group", axis=0, tiled=True),
        lax.all_gather(hidden, "group", axis=0, tiled=True),
    )
    partial_sums = (
        inner_t(normed_own, query_rows),
        inner_t(normed_own, key_rows),
        inner_t(normed_own, value_rows),
        inner_t(middle_own, mixed_rows),
        inner_t(normed_mlp_own, gate_rows),
        inner_t(normed_mlp_own, lift_rows),
        inner_t(top_own, hidden_rows),
    )
    grad_query, grad_key, grad_value, grad_out, grad_gate, grad_up, grad_down = (
        lax.psum_scatter(
            partial_sums[0].astype(jnp.bfloat16), "replica", scatter_dimension=0, tiled=True
        ).astype(jnp.float32),
        lax.psum_scatter(
            partial_sums[1].astype(jnp.bfloat16), "replica", scatter_dimension=0, tiled=True
        ).astype(jnp.float32),
        lax.psum_scatter(
            partial_sums[2].astype(jnp.bfloat16), "replica", scatter_dimension=0, tiled=True
        ).astype(jnp.float32),
        lax.psum_scatter(
            partial_sums[3].astype(jnp.bfloat16), "replica", scatter_dimension=0, tiled=True
        ).astype(jnp.float32),
        lax.psum_scatter(
            partial_sums[4].astype(jnp.bfloat16), "replica", scatter_dimension=0, tiled=True
        ).astype(jnp.float32),
        lax.psum_scatter(
            partial_sums[5].astype(jnp.bfloat16), "replica", scatter_dimension=0, tiled=True
        ).astype(jnp.float32),
        lax.psum_scatter(
            partial_sums[6].astype(jnp.bfloat16), "replica", scatter_dimension=0, tiled=True
        ).astype(jnp.float32),
    )
    gain_owned = lax.psum_scatter(
        jnp.stack([grad_gain_one, grad_gain_two]),
        ("group", "replica"),
        scatter_dimension=1,
        tiled=True,
    )
    squares = jnp.stack(
        [
            jnp.sum((source * source).reshape(sequences, -1), axis=1),
            jnp.sum((middle * middle).reshape(sequences, -1), axis=1),
            jnp.sum((output_full * output_full).reshape(sequences, -1), axis=1),
        ],
        axis=1,
    )
    square_totals = lax.psum(squares, "group")
    stream_rms = jnp.sqrt(square_totals / (full_len * model_width))
    layer_out = output_full.astype(jnp.bfloat16).reshape(sequences, block_size, model_width)
    input_grad = input_grad.reshape(sequences, block_size, model_width)
    return (
        layer_out,
        input_grad,
        gain_owned[0],
        grad_query,
        grad_key,
        grad_value,
        grad_out,
        gain_owned[1],
        grad_gate,
        grad_up,
        grad_down,
        stream_rms,
    )


def solution(mesh):
    placed = (
        P("replica", "group", None),
        P("replica", "group"),
        P("replica", None),
        P("group"),
        P("group", None),
        P("group", None),
        P("group", None),
        P("group", None),
        P("group"),
        P("group", None),
        P("group", None),
        P("group", None),
        P("replica", "group", None),
    )
    return jax.shard_map(
        shards,
        mesh=mesh,
        in_specs=placed,
        out_specs=(
            P("replica", "group", None),
            P("replica", "group", None),
            P(("group", "replica")),
            P(("group", "replica"), None),
            P(("group", "replica"), None),
            P(("group", "replica"), None),
            P(("group", "replica"), None),
            P(("group", "replica")),
            P(("group", "replica"), None),
            P(("group", "replica"), None),
            P(("group", "replica"), None),
            P("replica", None),
        ),
        check_vma=False,
    )
```

profile of v0, /device:TPU:0, one launch (start us, length us, event | category | flops | bytes accessed | tf_op | source)
XLA Modules:
  0.0 4407.7 jit_solution(10174914001787924033)
XLA Ops:
  27.3 50.7 %all-gather.24.cloned.1.call-done = bf16[2560,640]{1,0:T(8,128)(2,1)} async-done(((bf16[640,640]{1,0:T(8,128)(2,1)}), bf16[2560,640]{1,0:T(8,128)(2,1)}) %all-gather.24.cloned.1.call-update) | async-done | bytes 3276816 | tf_op jit(solution)/shard_map/all_gather | solution.py:91
  86.8 57.1 %all-gather.22.cloned.1.call-done = bf16[2560,640]{1,0:T(8,128)(2,1)} async-done(((bf16[640,640]{1,0:T(8,128)(2,1)}), bf16[2560,640]{1,0:T(8,128)(2,1)}) %all-gather.22.cloned.1.call-update) | async-done | bytes 3276816 | tf_op jit(solution)/shard_map/all_gather | solution.py:92
  179.2 32.1 all-gather.48.cloned.1.call-done
  213.7 224.8 %all-gather.26.cloned.1.call-done = bf16[2560,2560]{1,0:T(8,128)(2,1)} async-done(((bf16[640,2560]{1,0:T(8,128)(2,1)}), bf16[2560,2560]{1,0:T(8,128)(2,1)}) %all-gather.26.cloned.1.call-update) | async-done | bytes 13107216 | tf_op jit(solution)/shard_map/all_gather | solution.py:90
  489.3 175.7 %all-gather.28.cloned.1.call-done = bf16[2560,2560]{1,0:T(8,128)(2,1)} async-done(((bf16[640,2560]{1,0:T(8,128)(2,1)}), bf16[2560,2560]{1,0:T(8,128)(2,1)}) %all-gather.28.cloned.1.call-update) | async-done | bytes 13107216 | tf_op jit(solution)/shard_map/all_gather | solution.py:93
  673.9 605.2 %all-gather.30.cloned.1.call-done = bf16[2560,7168]{1,0:T(8,128)(2,1)} async-done(((bf16[640,7168]{1,0:T(8,128)(2,1)}), bf16[2560,7168]{1,0:T(8,128)(2,1)}) %all-gather.30.cloned.1.call-update) | async-done | bytes 36700176 | tf_op jit(solution)/shard_map/all_gather | solution.py:162
  1279.1 24.5 fusion.50
  1303.6 590.1 %all-gather.32.cloned.1.call-done = bf16[2560,7168]{1,0:T(8,128)(2,1)} async-done(((bf16[640,7168]{1,0:T(8,128)(2,1)}), bf16[2560,7168]{1,0:T(8,128)(2,1)}) %all-gather.32.cloned.1.call-update) | async-done | bytes 36700176 | tf_op jit(solution)/shard_map/all_gather | solution.py:163
  1893.7 24.5 fusion.51
  1918.3 590.1 %all-gather.34.cloned.1.call-done = bf16[2560,7168]{1,0:T(8,128)(2,1)} async-done(((bf16[640,7168]{1,0:T(8,128)(2,1)}), bf16[2560,7168]{1,0:T(8,128)(2,1)}) %all-gather.34.cloned.1.call-update) | async-done | bytes 36700176 | tf_op jit(solution)/shard_map/all_gather | solution.py:164
  2508.4 27.7 multiply_convert_fusion
  2554.6 21.0 multiply_reduce_fusion.1
  2606.1 22.3 fusion
  2628.4 28.1 fusion.2
  2671.6 48.2 %reduce-scatter.15.cloned.1.call-done = f32[1,256,640]{1,2,0:T(8,128)} async-done(((f32[1,1024,640]{1,2,0:T(8,128)}), f32[1,256,640]{1,2,0:T(8,128)}) %reduce-scatter.15.cloned.1.call-update) | async-done | bytes 655376 | tf_op jit(solution)/shard_map/reduce_scatter | solution.py:247
  2756.1 91.9 %all-gather.40.cloned.1.call-done = bf16[1024,2560]{0,1:T(8,128)(2,1)} async-done(((bf16[256,2560]{0,1:T(8,128)(2,1)}), bf16[1024,2560]{0,1:T(8,128)(2,1)}) %all-gather.40.cloned.1.call-update) | async-done | bytes 5242896 | tf_op jit(solution)/shard_map/all_gather | solution.py:279
  2861.0 51.0 %all_to_all.73 = bf16[256,4,640]{2,0,1:T(8,128)(2,1)S(1)} all-to-all(bf16[256,4,640]{2,0,1:T(8,128)(2,1)S(1)} %fusion.27), channel_id=1, replica_groups=mesh['group'=4,'replica'=8] {'group'}, dimensions={1} | all-to-all | bytes 2621440 | tf_op jit(solution)/shard_map/all_to_all | solution.py:270
  2915.5 24.7 all-gather.38.cloned.1.call-done
  2943.8 94.7 %all-gather.36.cloned.1.call-done = bf16[1024,2560]{0,1:T(8,128)(2,1)} async-done(((bf16[256,2560]{0,1:T(8,128)(2,1)}), bf16[1024,2560]{0,1:T(8,128)(2,1)}) %all-gather.36.cloned.1.call-update) | async-done | bytes 5242896 | tf_op jit(solution)/shard_map/all_gather | solution.py:276
  3049.3 76.3 %all_to_all.74 = bf16[256,4,640]{0,2,1:T(8,128)(2,1)S(1)} all-to-all(bf16[256,4,640]{0,2,1:T(8,128)(2,1)} %bitcast.221), channel_id=1, replica_groups=mesh['group'=4,'replica'=8] {'group'}, dimensions={1} | all-to-all | bytes 2621440 | tf_op jit(solution)/shard_map/all_to_all | solution.py:273
  3127.0 191.6 %all-gather.46.cloned.1.call-done = bf16[1024,7168]{1,0:T(8,128)(2,1)} async-done(((bf16[256,7168]{1,0:T(8,128)(2,1)}), bf16[1024,7168]{1,0:T(8,128)(2,1)}) %all-gather.46.cloned.1.call-update) | async-done | bytes 14680080 | tf_op jit(solution)/shard_map/all_gather | solution.py:284
  3350.5 75.0 %all_to_all.75 = bf16[256,4,640]{2,0,1:T(8,128)(2,1)S(1)} all-to-all(bf16[256,4,640]{2,0,1:T(8,128)(2,1)S(1)} %bitcast.220), channel_id=1, replica_groups=mesh['group'=4,'replica'=8] {'group'}, dimensions={1} | all-to-all | bytes 2621440 | tf_op jit(solution)/shard_map/all_to_all | solution.py:272
  3425.5 173.3 %all-gather.42.cloned.1.call-done = bf16[1024,7168]{1,0:T(8,128)(2,1)} async-done(((bf16[256,7168]{1,0:T(8,128)(2,1)}), bf16[1024,7168]{1,0:T(8,128)(2,1)}) %all-gather.42.cloned.1.call-update) | async-done | bytes 14680080 | tf_op jit(solution)/shard_map/all_gather | solution.py:282
  3616.4 234.5 %all-gather.44.cloned.1.call-done = bf16[1024,7168]{1,0:T(8,128)(2,1)} async-done(((bf16[256,7168]{1,0:T(8,128)(2,1)}), bf16[1024,7168]{1,0:T(8,128)(2,1)}) %all-gather.44.cloned.1.call-update) | async-done | bytes 14680080 | tf_op jit(solution)/shard_map/all_gather | solution.py:283
  3905.4 81.6 %reduce-scatter.31.cloned.1.call-done = f32[80,2]{1,0:T(8,128)} async-done(((f32[2560,2]{1,0:T(8,128)}), f32[80,2]{1,0:T(8,128)}) %reduce-scatter.31.cloned.1.call-update) | async-done | bytes 656
  3989.1 44.5 %reduce-scatter.25.cloned.1.call-done = bf16[80,2560]{1,0:T(8,128)(2,1)} async-done(((bf16[640,2560]{1,0:T(8,128)(2,1)}), bf16[80,2560]{1,0:T(8,128)(2,1)}) %reduce-scatter.25.cloned.1.call-update) | async-done | bytes 409616 | tf_op jit(solution)/shard_map/reduce_scatter | solution.py:305
  4035.5 36.8 reduce-scatter.23.cloned.1.call-done
  4073.9 36.8 reduce-scatter.21.cloned.1.call-done
  4112.4 49.1 %reduce-scatter.19.cloned.1.call-done = bf16[80,2560]{1,0:T(8,128)(2,1)} async-done(((bf16[640,2560]{1,0:T(8,128)(2,1)}), bf16[80,2560]{1,0:T(8,128)(2,1)}) %reduce-scatter.19.cloned.1.call-update) | async-done | bytes 409616 | tf_op jit(solution)/shard_map/reduce_scatter | solution.py:296
  4163.4 77.1 %reduce-scatter.33.cloned.1.call-done = bf16[80,7168]{1,0:T(8,128)(2,1)} async-done(((bf16[640,7168]{1,0:T(8,128)(2,1)}), bf16[80,7168]{1,0:T(8,128)(2,1)}) %reduce-scatter.33.cloned.1.call-update) | async-done | bytes 1146896
  4244.3 74.9 %reduce-scatter.27.cloned.1.call-done = bf16[80,7168]{1,0:T(8,128)(2,1)} async-done(((bf16[640,7168]{1,0:T(8,128)(2,1)}), bf16[80,7168]{1,0:T(8,128)(2,1)}) %reduce-scatter.27.cloned.1.call-update) | async-done | bytes 1146896 | tf_op jit(solution)/shard_map/reduce_scatter | solution.py:308
  4322.0 76.2 %reduce-scatter.29.cloned.1.call-done = bf16[80,7168]{1,0:T(8,128)(2,1)} async-done(((bf16[640,7168]{1,0:T(8,128)(2,1)}), bf16[80,7168]{1,0:T(8,128)(2,1)}) %reduce-scatter.29.cloned.1.call-update) | async-done | bytes 1146896 | tf_op jit(solution)/shard_map/reduce_scatter | solution.py:311
  (228 shorter events, 379.5 us)
Async XLA Ops:
  7.2 70.8 %all-gather.24.cloned.1.call-start = ((), (), s32[]{:S(2)}) async-start(), calls=%async_computation.15 | async-start | bytes 4096000 | tf_op jit(solution)/shard_map/all_gather | solution.py:91
  7.9 135.9 %all-gather.22.cloned.1.call-start = ((), (), s32[]{:S(2)}) async-start(), calls=%async_computation.14 | async-start | bytes 4096000 | tf_op jit(solution)/shard_map/all_gather | solution.py:92
  8.7 168.9 %all-gather.50.cloned.1.call-start = ((), (), s32[]{:S(2)}) async-start(), calls=%async_computation.36 | async-start | bytes 1638400 | tf_op jit(solution)/shard_map/all_gather | solution.py:121
  24.7 413.8 %copy-start.27 = (f32[2560]{0:T(1024)}, f32[2560]{0:T(1024)S(1)}, u32[]{:S(2)}) copy-start(f32[2560]{0:T(1024)S(1)} %reshape.535) | copy-start | bytes 30724
  25.8 421.4 %copy-start.22 = (f32[256,80]{0,1:T(8,128)}, f32[256,80]{0,1:T(8,128)S(1)}, u32[]{:S(2)}) copy-start(f32[256,80]{0,1:T(8,128)S(1)} %get-tuple-element.147) | copy-start | bytes 245764
  25.8 421.4 %copy-start.24 = (f32[256,80]{0,1:T(8,128)}, f32[256,80]{0,1:T(8,128)S(1)}, u32[]{:S(2)}) copy-start(f32[256,80]{0,1:T(8,128)S(1)} %get-tuple-element.148) | copy-start | bytes 245764
  86.8 124.5 %all-gather.48.cloned.1.call-start = ((), (), s32[]{:S(2)}) async-start(), calls=%async_computation.35 | async-start | bytes 1638400 | tf_op jit(solution)/shard_map/all_gather | solution.py:122
  147.8 290.7 %all-gather.26.cloned.1.call-start = ((), (), s32[]{:S(2)}) async-start(), calls=%async_computation.16 | async-start | bytes 16384000 | tf_op jit(solution)/shard_map/all_gather | solution.py:90
  148.4 516.5 %all-gather.28.cloned.1.call-start = ((), (), s32[]{:S(2)}) async-start(), calls=%async_computation.17 | async-start | bytes 16384000 | tf_op jit(solution)/shard_map/all_gather | solution.py:93
  149.0 1130.1 %all-gather.30.cloned.1.call-start = ((), (), s32[]{:S(2)}) async-start(), calls=%async_computation.18 | async-start | bytes 45875200 | tf_op jit(solution)/shard_map/all_gather | solution.py:162
  149.7 1744.0 %all-gather.32.cloned.1.call-start = ((), (), s32[]{:S(2)}) async-start(), calls=%async_computation.19 | async-start | bytes 45875200 | tf_op jit(solution)/shard_map/all_gather | solution.py:163
  150.5 2357.9 %all-gather.34.cloned.1.call-start = ((), (), s32[]{:S(2)}) async-start(), calls=%async_computation.20 | async-start | bytes 45875200 | tf_op jit(solution)/shard_map/all_gather | solution.py:164
  151.2 2518.5 %reduce-scatter.17.cloned.1.call-start = ((), (), s32[]{:S(2)}) async-start(), calls=%async_computation.22 | async-start | bytes 3276800 | tf_op jit(solution)/shard_map/reduce_scatter | solution.py:248
  673.9 1219.8 %copy-start.12 = (bf16[256,2560]{1,0:T(8,128)(2,1)}, bf16[256,2560]{1,0:T(8,128)(2,1)S(1)}, u32[]{:S(2)}) copy-start(bf16[256,2560]{1,0:T(8,128)(2,1)S(1)} %multiply_convert_fusion.3) | copy-start | bytes 3932164
  1303.6 1204.8 %copy-start.10 = (bf16[1,256,2560]{2,1,0:T(8,128)(2,1)S(1)}, bf16[1,256,2560]{2,1,0:T(8,128)(2,1)}, u32[]{:S(2)}) copy-start(bf16[1,256,2560]{2,1,0:T(8,128)(2,1)} %param.25) | copy-start | bytes 3932164
  2604.8 115.0 %reduce-scatter.15.cloned.1.call-start = ((), (), s32[]{:S(2)}) async-start(), calls=%async_computation.21 | async-start | bytes 3276800 | tf_op jit(solution)/shard_map/reduce_scatter | solution.py:247
  2669.0 178.9 %all-gather.40.cloned.1.call-start = ((), (), s32[]{:S(2)}) async-start(), calls=%async_computation.28 | async-start | bytes 6553600 | tf_op jit(solution)/shard_map/all_gather | solution.py:279
  2669.6 242.4 %all-gather.52.cloned.1.call-start = ((), (), s32[]{:S(2)}) async-start(), calls=%async_computation.37 | async-start | bytes 1638400 | tf_op jit(solution)/shard_map/all_gather | solution.py:278
  2671.6 268.7 %all-gather.38.cloned.1.call-start = ((), (), s32[]{:S(2)}) async-start(), calls=%async_computation.25 | async-start | bytes 1638400 | tf_op jit(solution)/shard_map/all_gather | solution.py:277
  2722.0 316.5 %all-gather.36.cloned.1.call-start = ((), (), s32[]{:S(2)}) async-start(), calls=%async_computation.23 | async-start | bytes 6553600 | tf_op jit(solution)/shard_map/all_gather | solution.py:276
  2733.8 584.8 %all-gather.46.cloned.1.call-start = ((), (), s32[]{:S(2)}) async-start(), calls=%async_computation.34 | async-start | bytes 18350080 | tf_op jit(solution)/shard_map/all_gather | solution.py:284
  2734.4 864.3 %all-gather.42.cloned.1.call-start = ((), (), s32[]{:S(2)}) async-start(), calls=%async_computation.30 | async-start | bytes 18350080 | tf_op jit(solution)/shard_map/all_gather | solution.py:282
  2735.0 1115.8 %all-gather.44.cloned.1.call-start = ((), (), s32[]{:S(2)}) async-start(), calls=%async_computation.32 | async-start | bytes 18350080 | tf_op jit(solution)/shard_map/all_gather | solution.py:283
  2737.5 110.5 %all-to-all-start.1 = ((bf16[256,4,640]{2,0,1:T(8,128)(2,1)}), bf16[256,4,640]{2,0,1:T(8,128)(2,1)}, u32[]{:S(2)}, u32[]{:S(2)}) async-start(bf16[256,4,640]{2,0,1:T(8,128)(2,1)} %bitcast.218), calls=%async_computation.6 | async-start | bytes 2621440 | tf_op jit(solution)/shard_map/all_to_all | solution.py:271
  2741.8 1245.2 %reduce-scatter.31.cloned.1.call-start = ((), (), s32[]{:S(2)}) async-start(), calls=%async_computation.38 | async-start | bytes 1351680
  2755.8 1277.8 %reduce-scatter.25.cloned.1.call-start = ((), (), s32[]{:S(2)}) async-start(), calls=%async_computation.29 | async-start | bytes 3686400 | tf_op jit(solution)/shard_map/reduce_scatter | solution.py:305
  2856.2 1216.2 %reduce-scatter.23.cloned.1.call-start = ((), (), s32[]{:S(2)}) async-start(), calls=%async_computation.27 | async-start | bytes 921600 | tf_op jit(solution)/shard_map/reduce_scatter | solution.py:302
  2915.5 1195.3 %reduce-scatter.21.cloned.1.call-start = ((), (), s32[]{:S(2)}) async-start(), calls=%async_computation.26 | async-start | bytes 921600 | tf_op jit(solution)/shard_map/reduce_scatter | solution.py:299
  2943.7 1217.8 %reduce-scatter.19.cloned.1.call-start = ((), (), s32[]{:S(2)}) async-start(), calls=%async_computation.24 | async-start | bytes 3686400 | tf_op jit(solution)/shard_map/reduce_scatter | solution.py:296
  3046.4 1194.1 %reduce-scatter.33.cloned.1.call-start = ((), (), s32[]{:S(2)}) async-start(), calls=%async_computation.39 | async-start | bytes 10321920
  3349.1 970.1 %reduce-scatter.27.cloned.1.call-start = ((), (), s32[]{:S(2)}) async-start(), calls=%async_computation.31 | async-start | bytes 10321920 | tf_op jit(solution)/shard_map/reduce_scatter | solution.py:308
  3616.1 782.0 %reduce-scatter.29.cloned.1.call-start = ((), (), s32[]{:S(2)}) async-start(), calls=%async_computation.33 | async-start | bytes 10321920 | tf_op jit(solution)/shard_map/reduce_scatter | solution.py:311
  (31 other events, 1134.6 us)
Sparse Core Ops, SparseCore 0:
  9.6 68.3 all-gather.23
  79.5 64.2 all-gather.21
  146.0 31.4 all-gather.49
  179.5 31.6 all-gather.47
  212.7 225.7 all-gather.25
  439.9 224.9 all-gather.27
  666.5 612.5 all-gather.29
  1280.6 613.0 all-gather.31
  1895.3 613.0 all-gather.33
  2604.9 50.8 reduce-scatter.16
  2669.2 50.5 reduce-scatter.14
  2721.2 126.6 all-gather.39
  2850.1 56.3 all-gather.51
  2908.5 31.7 all-gather.37
  2942.2 96.2 all-gather.35
  3039.9 278.6 all-gather.45
  3320.1 278.6 all-gather.41
  3600.2 250.6 all-gather.43
  3853.6 133.3 reduce-scatter.30
  3990.7 42.8 reduce-scatter.24
  4037.8 34.4 reduce-scatter.22
  4076.3 34.4 reduce-scatter.20
  4114.6 46.8 reduce-scatter.18
  4165.4 75.0 reduce-scatter.32
  4244.1 75.0 reduce-scatter.26
  4323.1 75.0 reduce-scatter.28
where the time goes:
time: 4410 us
  waiting for transfers between devices  3680 us (83%)
  matrix products  341 us (8%)
  blocking collectives  239 us (5%)
  other arithmetic  83.8 us (2%)
  local copies, waits for them, and re-layouts  45.3 us (1%)
    all_gather x1, waiting for transfers between devices, shards(): gate_piece = lax.all_gather(w_gate, 'group', axis=0, tiled=True)  605 us
    all_gather x1, waiting for transfers between devices, shards(): down_piece = lax.all_gather(w_down, 'group', axis=0, tiled=True)  590 us
    all_gather x1, waiting for transfers between devices, shards(): up_piece = lax.all_gather(w_up, 'group', axis=0, tiled=True)  590 us
    all_gather x1, waiting for transfers between devices, shards(): lax.all_gather(grad_lift_low, 'group', axis=0, tiled=True)  234 us
    all_gather x1, waiting for transfers between devices, shards(): query_piece = lax.all_gather(w_query, 'group', axis=0, tiled=True)  225 us
    all_gather x1, waiting for transfers between devices, shards(): lax.all_gather(hidden, 'group', axis=0, tiled=True)  192 us
    all_gather x1, waiting for transfers between devices, shards(): out_piece = lax.all_gather(w_out, 'group', axis=0, tiled=True)  176 us
    all_gather x1, waiting for transfers between devices, shards(): lax.all_gather(grad_gate_low, 'group', axis=0, tiled=True)  173 us
  transfers between devices with their start and end apart: 27, of which 24 were waited for; matrix products, arithmetic and copies ran while one was open for 8% of the time, Pallas kernels for 0%

commit v1 on v0

--- a/solution.py
+++ b/solution.py
@@ -77,6 +77,21 @@
     w_down,
     out_grad,
 ):
+
+    def face_convert(my_data, ax_name):
+        how_many = lax.axis_size(ax_name)
+        pieces_in = [(ii, (ii + 1) % how_many) for ii in range(how_many)]
+
+        def apply_the_sums_all(all_values):
+            if len(all_values) == how_many:
+                return all_values
+            return apply_the_sums_all(
+                [lax.ppermute(all_values[0], axis_name=ax_name, perm=pieces_in), *all_values]
+            )
+
+        passed = jnp.concatenate(apply_the_sums_all([my_data]), 0)
+        return jnp.roll(passed, (lax.axis_index(ax_name) + 1) * my_data.shape[0], 0)
+
     sequences, block_size, model_width = layer_input.shape
     token_rows = sequences * block_size
     kv_width = KV_HEADS * HEAD_DIM
@@ -159,7 +174,7 @@
     inverse_two = inverse_rms(middle)
     unit_two = middle * inverse_two
     gain_piece = lax.all_gather(gain_mlp, "group", axis=0, tiled=True)
-    gate_piece = lax.all_gather(w_gate, "group", axis=0, tiled=True)
+    gate_piece = face_convert(w_gate, ax_name="group")
     up_piece = lax.all_gather(w_up, "group", axis=0, tiled=True)
     down_piece = lax.all_gather(w_down, "group", axis=0, tiled=True)
     scaled = unit_two * gain_piece.astype(jnp.float32)

time: 4410 us -> 4920 us (1.12)
  blocking collectives: 239 us -> 639 us
  starting transfers between devices: 5.94 us -> 88.2 us
  local copies, waits for them, and re-layouts: 45.3 us -> 108 us
    ppermute x0 -> x3, waiting for transfers between devices: none -> 697 us  [apply_the_sums_all(): lax.ppermute(all_values[0], axis_name=ax_name, perm=pieces_in)]
    all_gather x1, blocking collectives: 13.6 us -> 414 us  [shards(): gain_piece = lax.all_gather(gain_mlp, 'group', axis=0, tiled=True)]
    all_gather x1, waiting for transfers between devices: 590 us -> 336 us  [shards(): up_piece = lax.all_gather(w_up, 'group', axis=0, tiled=True)]
    all_gather x1, waiting for transfers between devices: 225 us -> 0.01 us  [shards(): query_piece = lax.all_gather(w_query, 'group', axis=0, tiled=True)]
    all_gather x1, waiting for transfers between devices: 176 us -> 0.02 us  [shards(): out_piece = lax.all_gather(w_out, 'group', axis=0, tiled=True)]
    ppermute x0 -> x3, starting transfers between devices: none -> 82.4 us  [apply_the_sums_all(): lax.ppermute(all_values[0], axis_name=ax_name, perm=pieces_in)]
    unnamed x82 -> x93, local copies, waits for them, and re-layouts: 31.5 us -> 84.8 us
  transfers between devices with their start and end apart: 27 -> 30, of which waited for: 24 -> 22; matrix products, arithmetic and copies ran while one was open for 8% -> 9% of each run, Pallas kernels for 0% -> 0%
where the time goes in v1:
time: 4920 us
  waiting for transfers between devices  3640 us (74%)
  blocking collectives  639 us (13%)
  matrix products  343 us (7%)
  local copies, waits for them, and re-layouts  108 us (2%)
  starting transfers between devices  88.2 us (2%)
  other arithmetic  85.3 us (2%)
    ppermute x3, waiting for transfers between devices, apply_the_sums_all(): lax.ppermute(all_values[0], axis_name=ax_name, perm=pieces_in)  697 us
    all_gather x1, waiting for transfers between devices, shards(): down_piece = lax.all_gather(w_down, 'group', axis=0, tiled=True)  590 us
    all_gather x1, waiting for transfers between devices, shards(): gate_piece = lax.all_gather(w_gate, 'group', axis=0, tiled=True)  562 us
    all_gather x1, blocking collectives, shards(): gain_piece = lax.all_gather(gain_mlp, 'group', axis=0, tiled=True)  414 us
    all_gather x1, waiting for transfers between devices, shards(): up_piece = lax.all_gather(w_up, 'group', axis=0, tiled=True)  336 us
    all_gather x1, waiting for transfers between devices, shards(): lax.all_gather(grad_lift_low, 'group', axis=0, tiled=True)  234 us
    all_gather x1, waiting for transfers between devices, shards(): lax.all_gather(hidden, 'group', axis=0, tiled=True)  192 us
    all_gather x1, waiting for transfers between devices, shards(): lax.all_gather(grad_gate_low, 'group', axis=0, tiled=True)  173 us
  transfers between devices with their start and end apart: 30, of which 22 were waited for; matrix products, arithmetic and copies ran while one was open for 9% of the time, Pallas kernels for 0%

profile of v1, /device:TPU:0, one launch (start us, length us, event | category | flops | bytes accessed | tf_op | source)
XLA Modules:
  0.0 4915.6 jit_solution(17902910795167082891)
XLA Ops:
  27.3 50.6 %all-gather.24.cloned.1.call-done = bf16[2560,640]{1,0:T(8,128)(2,1)} async-done(((bf16[640,640]{1,0:T(8,128)(2,1)}), bf16[2560,640]{1,0:T(8,128)(2,1)}) %all-gather.24.cloned.1.call-update) | async-done | bytes 3276816 | tf_op jit(solution)/shard_map/all_gather | solution.py:106
  86.8 57.1 %all-gather.22.cloned.1.call-done = bf16[2560,640]{1,0:T(8,128)(2,1)} async-done(((bf16[640,640]{1,0:T(8,128)(2,1)}), bf16[2560,640]{1,0:T(8,128)(2,1)}) %all-gather.22.cloned.1.call-update) | async-done | bytes 3276816 | tf_op jit(solution)/shard_map/all_gather | solution.py:107
  151.3 369.6 %collective-permute-done = bf16[640,7168]{1,0:T(8,128)(2,1)} collective-permute-done((bf16[640,7168]{1,0:T(8,128)(2,1)}, bf16[640,7168]{1,0:T(8,128)(2,1)}, u32[]{:S(2)}, u32[]{:S(2)}) %collective-permute-start) | collective-permute-done | bytes 9175072 | tf_op jit(solution)/shard_map/ppermute | solution.py:89
  521.0 81.6 %collective-permute-start.1 = (bf16[640,7168]{1,0:T(8,128)(2,1)}, bf16[640,7168]{1,0:T(8,128)(2,1)}, u32[]{:S(2)}, u32[]{:S(2)}) collective-permute-start(bf16[640,7168]{1,0:T(8,128)(2,1)} %collective-permute-done), channel_id=1, source_target_pairs={{0,8},{8,16},{16,24},{24,0},{1,9},{9,17},{17,25},{25,1},{2,10},{10... | collective-permute-start | bytes 27525128 | tf_op jit(solution)/shard_map/ppermute | solution.py:89
  604.5 413.9 %all-gather.4 = bf16[4,1,640]{2,1,0:T(2,128)(2,1)S(1)} all-gather(bf16[1,1,640]{2,1,0:T(2,128)(2,1)S(1)} %reshape.533), channel_id=1, replica_groups=mesh['group'=4,'replica'=8] {'group'}, dimensions={0}, use_global_device_ids=true | all-gather | bytes 6400 | tf_op jit(solution)/shard_map/all_gather | solution.py:176
  1088.9 327.2 %collective-permute-done.2 = bf16[640,7168]{1,0:T(8,128)(2,1)} collective-permute-done((bf16[640,7168]{1,0:T(8,128)(2,1)}, bf16[640,7168]{1,0:T(8,128)(2,1)}, u32[]{:S(2)}, u32[]{:S(2)}) %collective-permute-start.2) | collective-permute-done | bytes 9175072 | tf_op jit(solution)/shard_map/ppermute | solution.py:89
  1478.6 335.8 %all-gather.30.cloned.1.call-done = bf16[2560,7168]{1,0:T(8,128)(2,1)} async-done(((bf16[640,7168]{1,0:T(8,128)(2,1)}), bf16[2560,7168]{1,0:T(8,128)(2,1)}) %all-gather.30.cloned.1.call-update) | async-done | bytes 36700176 | tf_op jit(solution)/shard_map/all_gather | solution.py:178
  1814.4 24.7 fusion.53
  1839.1 589.8 %all-gather.32.cloned.1.call-done = bf16[2560,7168]{1,0:T(8,128)(2,1)} async-done(((bf16[640,7168]{1,0:T(8,128)(2,1)}), bf16[2560,7168]{1,0:T(8,128)(2,1)}) %all-gather.32.cloned.1.call-update) | async-done | bytes 36700176 | tf_op jit(solution)/shard_map/all_gather | solution.py:179
  2428.9 24.8 fusion.32
  2453.7 27.5 multiply_convert_fusion
  2481.2 562.4 %all-gather.34.cloned.1.call-done = bf16[2560,7168]{1,0:T(8,128)(2,1)} async-done(((bf16[640,7168]{1,0:T(8,128)(2,1)}), bf16[2560,7168]{1,0:T(8,128)(2,1)}) %all-gather.34.cloned.1.call-update) | async-done | bytes 36700176 | tf_op jit(solution)/shard_map/all_gather | solution.py:200
  3113.6 22.8 fusion.2
  3136.4 28.1 fusion.4
  3179.5 48.2 reduce-scatter.15.cloned.1.call-done
  3263.9 91.9 %all-gather.40.cloned.1.call-done = bf16[1024,2560]{0,1:T(8,128)(2,1)} async-done(((bf16[256,2560]{0,1:T(8,128)(2,1)}), bf16[1024,2560]{0,1:T(8,128)(2,1)}) %all-gather.40.cloned.1.call-update) | async-done | bytes 5242896 | tf_op jit(solution)/shard_map/all_gather | solution.py:294
  3368.8 50.8 %all_to_all.73 = bf16[256,4,640]{2,0,1:T(8,128)(2,1)S(1)} all-to-all(bf16[256,4,640]{2,0,1:T(8,128)(2,1)S(1)} %fusion.29), channel_id=1, replica_groups=mesh['group'=4,'replica'=8] {'group'}, dimensions={1} | all-to-all | bytes 2621440 | tf_op jit(solution)/shard_map/all_to_all | solution.py:285
  3423.4 24.5 all-gather.38.cloned.1.call-done
  3451.4 94.7 %all-gather.36.cloned.1.call-done = bf16[1024,2560]{0,1:T(8,128)(2,1)} async-done(((bf16[256,2560]{0,1:T(8,128)(2,1)}), bf16[1024,2560]{0,1:T(8,128)(2,1)}) %all-gather.36.cloned.1.call-update) | async-done | bytes 5242896 | tf_op jit(solution)/shard_map/all_gather | solution.py:291
  3556.9 76.4 %all_to_all.74 = bf16[256,4,640]{0,2,1:T(8,128)(2,1)S(1)} all-to-all(bf16[256,4,640]{0,2,1:T(8,128)(2,1)} %bitcast.218), channel_id=1, replica_groups=mesh['group'=4,'replica'=8] {'group'}, dimensions={1} | all-to-all | bytes 2621440 | tf_op jit(solution)/shard_map/all_to_all | solution.py:288
  3634.7 191.6 %all-gather.46.cloned.1.call-done = bf16[1024,7168]{1,0:T(8,128)(2,1)} async-done(((bf16[256,7168]{1,0:T(8,128)(2,1)}), bf16[1024,7168]{1,0:T(8,128)(2,1)}) %all-gather.46.cloned.1.call-update) | async-done | bytes 14680080 | tf_op jit(solution)/shard_map/all_gather | solution.py:299
  3858.1 75.1 %all_to_all.75 = bf16[256,4,640]{2,0,1:T(8,128)(2,1)S(1)} all-to-all(bf16[256,4,640]{2,0,1:T(8,128)(2,1)S(1)} %bitcast.217), channel_id=1, replica_groups=mesh['group'=4,'replica'=8] {'group'}, dimensions={1} | all-to-all | bytes 2621440 | tf_op jit(solution)/shard_map/all_to_all | solution.py:287
  3933.1 173.3 %all-gather.42.cloned.1.call-done = bf16[1024,7168]{1,0:T(8,128)(2,1)} async-done(((bf16[256,7168]{1,0:T(8,128)(2,1)}), bf16[1024,7168]{1,0:T(8,128)(2,1)}) %all-gather.42.cloned.1.call-update) | async-done | bytes 14680080 | tf_op jit(solution)/shard_map/all_gather | solution.py:297
  4124.1 234.4 %all-gather.44.cloned.1.call-done = bf16[1024,7168]{1,0:T(8,128)(2,1)} async-done(((bf16[256,7168]{1,0:T(8,128)(2,1)}), bf16[1024,7168]{1,0:T(8,128)(2,1)}) %all-gather.44.cloned.1.call-update) | async-done | bytes 14680080 | tf_op jit(solution)/shard_map/all_gather | solution.py:298
  4413.0 81.7 %reduce-scatter.31.cloned.1.call-done = f32[80,2]{1,0:T(8,128)} async-done(((f32[2560,2]{1,0:T(8,128)}), f32[80,2]{1,0:T(8,128)}) %reduce-scatter.31.cloned.1.call-update) | async-done | bytes 656
  4496.8 44.4 reduce-scatter.25.cloned.1.call-done
  4543.2 36.8 reduce-scatter.23.cloned.1.call-done
  4581.6 36.9 reduce-scatter.21.cloned.1.call-done
  4620.1 49.1 reduce-scatter.19.cloned.1.call-done
  4671.1 77.1 %reduce-scatter.33.cloned.1.call-done = bf16[80,7168]{1,0:T(8,128)(2,1)} async-done(((bf16[640,7168]{1,0:T(8,128)(2,1)}), bf16[80,7168]{1,0:T(8,128)(2,1)}) %reduce-scatter.33.cloned.1.call-update) | async-done | bytes 1146896
  4751.9 74.9 %reduce-scatter.27.cloned.1.call-done = bf16[80,7168]{1,0:T(8,128)(2,1)} async-done(((bf16[640,7168]{1,0:T(8,128)(2,1)}), bf16[80,7168]{1,0:T(8,128)(2,1)}) %reduce-scatter.27.cloned.1.call-update) | async-done | bytes 1146896 | tf_op jit(solution)/shard_map/reduce_scatter | solution.py:323
  4829.7 76.2 %reduce-scatter.29.cloned.1.call-done = bf16[80,7168]{1,0:T(8,128)(2,1)} async-done(((bf16[640,7168]{1,0:T(8,128)(2,1)}), bf16[80,7168]{1,0:T(8,128)(2,1)}) %reduce-scatter.29.cloned.1.call-update) | async-done | bytes 1146896 | tf_op jit(solution)/shard_map/reduce_scatter | solution.py:326
  (246 shorter events, 445.1 us)
Async XLA Ops:
  7.2 70.8 %all-gather.24.cloned.1.call-start = ((), (), s32[]{:S(2)}) async-start(), calls=%async_computation.15 | async-start | bytes 4096000 | tf_op jit(solution)/shard_map/all_gather | solution.py:106
  7.9 136.0 %all-gather.22.cloned.1.call-start = ((), (), s32[]{:S(2)}) async-start(), calls=%async_computation.14 | async-start | bytes 4096000 | tf_op jit(solution)/shard_map/all_gather | solution.py:107
  8.7 1012.9 %all-gather.50.cloned.1.call-start = ((), (), s32[]{:S(2)}) async-start(), calls=%async_computation.36 | async-start | bytes 1638400 | tf_op jit(solution)/shard_map/all_gather | solution.py:136
  25.8 1011.8 %copy-start.22 = (f32[256,80]{0,1:T(8,128)}, f32[256,80]{0,1:T(8,128)S(1)}, u32[]{:S(2)}) copy-start(f32[256,80]{0,1:T(8,128)S(1)} %get-tuple-element.147) | copy-start | bytes 245764
  86.8 936.9 %all-gather.48.cloned.1.call-start = ((), (), s32[]{:S(2)}) async-start(), calls=%async_computation.35 | async-start | bytes 1638400 | tf_op jit(solution)/shard_map/all_gather | solution.py:137
  147.8 879.7 %all-gather.26.cloned.1.call-start = ((), (), s32[]{:S(2)}) async-start(), calls=%async_computation.16 | async-start | bytes 16384000 | tf_op jit(solution)/shard_map/all_gather | solution.py:105
  148.4 931.0 %all-gather.28.cloned.1.call-start = ((), (), s32[]{:S(2)}) async-start(), calls=%async_computation.17 | async-start | bytes 16384000 | tf_op jit(solution)/shard_map/all_gather | solution.py:108
  149.0 1665.5 %all-gather.30.cloned.1.call-start = ((), (), s32[]{:S(2)}) async-start(), calls=%async_computation.18 | async-start | bytes 45875200 | tf_op jit(solution)/shard_map/all_gather | solution.py:178
  149.7 2279.2 %all-gather.32.cloned.1.call-start = ((), (), s32[]{:S(2)}) async-start(), calls=%async_computation.19 | async-start | bytes 45875200 | tf_op jit(solution)/shard_map/all_gather | solution.py:179
  150.5 2893.1 %all-gather.34.cloned.1.call-start = ((), (), s32[]{:S(2)}) async-start(), calls=%async_computation.20 | async-start | bytes 45875200 | tf_op jit(solution)/shard_map/all_gather | solution.py:200
  151.2 3026.4 %reduce-scatter.17.cloned.1.call-start = ((), (), s32[]{:S(2)}) async-start(), calls=%async_computation.22 | async-start | bytes 3276800 | tf_op jit(solution)/shard_map/reduce_scatter | solution.py:263
  151.3 369.7 %collective-permute-start = (bf16[640,7168]{1,0:T(8,128)(2,1)}, bf16[640,7168]{1,0:T(8,128)(2,1)}, u32[]{:S(2)}, u32[]{:S(2)}) collective-permute-start(bf16[640,7168]{1,0:T(8,128)(2,1)} %param.22), channel_id=1, source_target_pairs={{0,8},{8,16},{16,24},{24,0},{1,9},{9,17},{17,25},{25,1},{2,10},{10... | collective-permute-start | bytes 27525128 | tf_op jit(solution)/shard_map/ppermute | solution.py:89
  521.0 505.8 %collective-permute-start.1 = (bf16[640,7168]{1,0:T(8,128)(2,1)}, bf16[640,7168]{1,0:T(8,128)(2,1)}, u32[]{:S(2)}, u32[]{:S(2)}) collective-permute-start(bf16[640,7168]{1,0:T(8,128)(2,1)} %collective-permute-done), channel_id=1, source_target_pairs={{0,8},{8,16},{16,24},{24,0},{1,9},{9,17},{17,25},{25,1},{2,10},{10... | collective-permute-start | bytes 27525128 | tf_op jit(solution)/shard_map/ppermute | solution.py:89
  1026.8 389.3 %collective-permute-start.2 = (bf16[640,7168]{1,0:T(8,128)(2,1)}, bf16[640,7168]{1,0:T(8,128)(2,1)}, u32[]{:S(2)}, u32[]{:S(2)}) collective-permute-start(bf16[640,7168]{1,0:T(8,128)(2,1)} %collective-permute-done.1), channel_id=1, source_target_pairs={{0,8},{8,16},{16,24},{24,0},{1,9},{9,17},{17,25},{25,1},{2,10},{10... | collective-permute-start | bytes 27525128 | tf_op jit(solution)/shard_map/ppermute | solution.py:89
  1088.9 1364.8 %copy-start.12 = (bf16[256,2560]{1,0:T(8,128)(2,1)}, bf16[256,2560]{1,0:T(8,128)(2,1)S(1)}, u32[]{:S(2)}) copy-start(bf16[256,2560]{1,0:T(8,128)(2,1)S(1)} %multiply_convert_fusion.3) | copy-start | bytes 3932164
  3112.3 115.4 %reduce-scatter.15.cloned.1.call-start = ((), (), s32[]{:S(2)}) async-start(), calls=%async_computation.21 | async-start | bytes 3276800 | tf_op jit(solution)/shard_map/reduce_scatter | solution.py:262
  3176.9 178.9 %all-gather.40.cloned.1.call-start = ((), (), s32[]{:S(2)}) async-start(), calls=%async_computation.28 | async-start | bytes 6553600 | tf_op jit(solution)/shard_map/all_gather | solution.py:294
  3177.5 242.1 %all-gather.52.cloned.1.call-start = ((), (), s32[]{:S(2)}) async-start(), calls=%async_computation.37 | async-start | bytes 1638400 | tf_op jit(solution)/shard_map/all_gather | solution.py:293
  3179.5 268.5 %all-gather.38.cloned.1.call-start = ((), (), s32[]{:S(2)}) async-start(), calls=%async_computation.25 | async-start | bytes 1638400 | tf_op jit(solution)/shard_map/all_gather | solution.py:292
  3229.9 316.2 %all-gather.36.cloned.1.call-start = ((), (), s32[]{:S(2)}) async-start(), calls=%async_computation.23 | async-start | bytes 6553600 | tf_op jit(solution)/shard_map/all_gather | solution.py:291
  3241.7 584.6 %all-gather.46.cloned.1.call-start = ((), (), s32[]{:S(2)}) async-start(), calls=%async_computation.34 | async-start | bytes 18350080 | tf_op jit(solution)/shard_map/all_gather | solution.py:299
  3242.3 864.1 %all-gather.42.cloned.1.call-start = ((), (), s32[]{:S(2)}) async-start(), calls=%async_computation.30 | async-start | bytes 18350080 | tf_op jit(solution)/shard_map/all_gather | solution.py:297
  3242.9 1115.6 %all-gather.44.cloned.1.call-start = ((), (), s32[]{:S(2)}) async-start(), calls=%async_computation.32 | async-start | bytes 18350080 | tf_op jit(solution)/shard_map/all_gather | solution.py:298
  3245.4 110.5 %all-to-all-start.1 = ((bf16[256,4,640]{2,0,1:T(8,128)(2,1)}), bf16[256,4,640]{2,0,1:T(8,128)(2,1)}, u32[]{:S(2)}, u32[]{:S(2)}) async-start(bf16[256,4,640]{2,0,1:T(8,128)(2,1)} %bitcast.215), calls=%async_computation.6 | async-start | bytes 2621440 | tf_op jit(solution)/shard_map/all_to_all | solution.py:286
  3249.7 1245.0 %reduce-scatter.31.cloned.1.call-start = ((), (), s32[]{:S(2)}) async-start(), calls=%async_computation.38 | async-start | bytes 1351680
  3263.9 1277.3 %reduce-scatter.25.cloned.1.call-start = ((), (), s32[]{:S(2)}) async-start(), calls=%async_computation.29 | async-start | bytes 3686400 | tf_op jit(solution)/shard_map/reduce_scatter | solution.py:320
  3364.1 1215.9 %reduce-scatter.23.cloned.1.call-start = ((), (), s32[]{:S(2)}) async-start(), calls=%async_computation.27 | async-start | bytes 921600 | tf_op jit(solution)/shard_map/reduce_scatter | solution.py:317
  3423.2 1195.3 %reduce-scatter.21.cloned.1.call-start = ((), (), s32[]{:S(2)}) async-start(), calls=%async_computation.26 | async-start | bytes 921600 | tf_op jit(solution)/shard_map/reduce_scatter | solution.py:314
  3451.4 1217.8 %reduce-scatter.19.cloned.1.call-start = ((), (), s32[]{:S(2)}) async-start(), calls=%async_computation.24 | async-start | bytes 3686400 | tf_op jit(solution)/shard_map/reduce_scatter | solution.py:311
  3554.0 1194.2 %reduce-scatter.33.cloned.1.call-start = ((), (), s32[]{:S(2)}) async-start(), calls=%async_computation.39 | async-start | bytes 10321920
  3856.7 970.2 %reduce-scatter.27.cloned.1.call-start = ((), (), s32[]{:S(2)}) async-start(), calls=%async_computation.31 | async-start | bytes 10321920 | tf_op jit(solution)/shard_map/reduce_scatter | solution.py:323
  4123.8 782.0 %reduce-scatter.29.cloned.1.call-start = ((), (), s32[]{:S(2)}) async-start(), calls=%async_computation.33 | async-start | bytes 10321920 | tf_op jit(solution)/shard_map/reduce_scatter | solution.py:326
  (36 other events, 5183.8 us)
Sparse Core Ops, SparseCore 0:
  9.6 68.3 all-gather.23
  79.5 64.2 all-gather.21
  146.0 53.1 all-gather.49
  201.3 52.9 all-gather.47
  255.7 350.3 all-gather.25
  607.5 405.5 all-gather.27
  1014.7 799.6 all-gather.29
  1816.0 612.8 all-gather.31
  2430.5 613.0 all-gather.33
  3112.4 50.8 reduce-scatter.16
  3177.1 50.6 reduce-scatter.14
  3229.1 126.7 all-gather.39
  3358.0 56.1 all-gather.51
  3416.2 31.6 all-gather.37
  3449.9 96.2 all-gather.35
  3547.6 278.6 all-gather.45
  3827.7 278.6 all-gather.41
  4107.8 250.6 all-gather.43
  4361.3 133.3 reduce-scatter.30
  4498.4 42.7 reduce-scatter.24
  4545.5 34.4 reduce-scatter.22
  4583.9 34.4 reduce-scatter.20
  4622.3 46.8 reduce-scatter.18
  4673.1 75.0 reduce-scatter.32
  4751.8 75.0 reduce-scatter.26
  4830.8 75.0 reduce-scatter.28
